TPU v7x, 32 devices: a whole 2x2x4 slice. The times are simulated.
32 devices in a mesh: sp: 4 (over z), bn: 2 (over x), dp: 4 (over y, core).
Axes of the slice: x: 2, y: 2, z: 4, core: 2. Of those that a mesh axis runs over, the one named last changes fastest.
Arguments:
- images: bfloat16 [8, 4, 64, 40, 128], P(('bn', 'dp'), 'sp'), may hold values from -8 to 8, as said below
- out_grad: bfloat16 [8, 4, 256, 40, 128], P(('bn', 'dp'), 'sp'), may hold values from -8 to 8, as said below
- conv_weight: bfloat16 [3, 3, 64, 64], replicated, may hold values from -0.25 to 0.25
- proj_weight: bfloat16 [64, 256], replicated, may hold values from -0.75 to 0.75
- gain_one: float32 [64], replicated, may hold values from 0.1 to 1.9
- shift_one: float32 [64], replicated, may hold values from -3 to 3
- gain_three: float32 [256], replicated, may hold values from 0.1 to 1.9
- shift_three: float32 [256], replicated, may hold values from -3 to 3
Outputs:
- images_grad: bfloat16 [8, 4, 64, 40, 128], P(('bn', 'dp'), 'sp')
- conv_grad: float32 [3, 3, 64, 64], replicated
- proj_grad: float32 [64, 256], replicated
- gain_one_grad: float32 [64], replicated
- shift_one_grad: float32 [64], replicated
- gain_three_grad: float32 [256], replicated
- shift_three_grad: float32 [256], replicated
Inputs may be any that keep to these rules, and one draw needn't show every extreme that they name: `images`: channels of one quadrant have their own offset and spread. `out_grad`: channels of one quadrant have their own offset and spread.
All inputs are finite; a program needn't handle non-finite values.
Results may differ from a plain program's by a relative error of at most 0.029.
Values may be sent and summed in bfloat16 or wider, within the bound.
A program may use at most 64 MiB of HBM per device.

v0:
```python
import jax
import jax.numpy as jnp
from jax import lax
from jax.sharding import PartitionSpec as P

norm_floor = 1e-05


def from_partner(value, axis, distance):
    return lax.ppermute(value, axis, [(i, i ^ 1 << distance) for i in range(lax.axis_size(axis))])


def combined_all(value, axis, combine):
    everything = jax.tree.map(lambda part: lax.all_gather(part, axis), value)
    initial = jax.tree.map(lambda part: part[0], everything)

    def turn(k, so_far):
        return combine(so_far, jax.tree.map(lambda part: part[k], everything))

    return lax.fori_loop(1, lax.axis_size(axis), turn, initial)


def silu_slope(inputs):
    sigma = jax.nn.sigmoid(inputs)
    return sigma * (1.0 + inputs * (1.0 - sigma))


def channel(vector):
    return vector[None, :, None, None]


def extend(field):
    position = lax.axis_index("sp")
    column = position % 2
    row_half = position // 2
    edge_cols = jnp.where(column == 0, field[:, :, :, -1:], field[:, :, :, :1])
    across = from_partner(edge_cols, "sp", 0)
    empty_cols = jnp.zeros_like(across)
    left_side = jnp.where(column == 1, across, empty_cols)
    right_side = jnp.where(column == 0, across, empty_cols)
    wider = jnp.concatenate([left_side, field, right_side], axis=3)
    edge_rows = jnp.where(row_half == 0, wider[:, :, -1:, :], wider[:, :, :1, :])
    incoming = from_partner(edge_rows, "sp", 1)
    empty_rows = jnp.zeros_like(incoming)
    top_side = jnp.where(row_half == 1, incoming, empty_rows)
    bottom_side = jnp.where(row_half == 0, incoming, empty_rows)
    return jnp.concatenate([top_side, wider, bottom_side], axis=2)


def conv_cells(padded, kernel, tile_rows, tile_cols):
    summed = None
    for row_off in range(3):
        for col_off in range(3):
            window = padded[:, :, row_off : row_off + tile_rows, col_off : col_off + tile_cols]
            partial_sum = jnp.einsum(
                "oi,nihw->nohw",
                kernel[row_off, col_off],
                window,
                preferred_element_type=jnp.float32,
            )
            summed = partial_sum if summed is None else summed + partial_sum
    return summed


def conv_back(padded, kernel, tile_rows, tile_cols):
    summed = None
    for row_off in range(3):
        for col_off in range(3):
            window = padded[
                :, :, 2 - row_off : 2 - row_off + tile_rows, 2 - col_off : 2 - col_off + tile_cols
            ]
            partial_sum = jnp.einsum(
                "oi,nohw->nihw",
                kernel[row_off, col_off],
                window,
                preferred_element_type=jnp.float32,
            )
            summed = partial_sum if summed is None else summed + partial_sum
    return summed


def kernel_grad(padded, grad_conv_out, tile_rows, tile_cols):
    pieces_list = []
    for row_off in range(3):
        for col_off in range(3):
            window = padded[:, :, row_off : row_off + tile_rows, col_off : col_off + tile_cols]
            pieces_list.append(
                jnp.einsum(
                    "nohw,nihw->oi", grad_conv_out, window, preferred_element_type=jnp.float32
                )
            )
    depth = grad_conv_out.shape[1]
    return jnp.stack(pieces_list).reshape(3, 3, depth, depth)


def chan_join(first, second):
    count_first, mean_first, square_first = first
    count_second, mean_second, square_second = second
    joined = count_first + count_second
    delta_mean = mean_second - mean_first
    share = count_second / joined
    return (
        joined,
        mean_first + delta_mean * share,
        square_first + square_second + delta_mean * delta_mean * count_first * share,
    )


def group_moments(values, cell_count):
    local_cells = float(values.shape[0] * values.shape[2] * values.shape[3])
    local_mean = jnp.mean(values, axis=(0, 2, 3))
    centred = values - channel(local_mean)
    local_square = jnp.sum(centred * centred, axis=(0, 2, 3))
    counts = jnp.full(local_mean.shape, local_cells, jnp.float32)
    merged = combined_all((counts, local_mean, local_square), ("sp", "bn"), chan_join)
    average = merged[1]
    squares = merged[2]
    return (average, squares / cell_count)


def norm_backward(grad_pre, normed, gain, scale, cell_count):
    local_sum = jnp.sum(grad_pre, axis=(0, 2, 3))
    local_cross = jnp.sum(grad_pre * normed, axis=(0, 2, 3))
    group_sum, group_cross = lax.psum((local_sum, local_cross), ("sp", "bn"))
    grad_in = channel(gain * scale) * (
        grad_pre - channel(group_sum) / cell_count - normed * channel(group_cross) / cell_count
    )
    return (grad_in.astype(jnp.bfloat16), local_sum, local_cross, group_sum, group_cross)


def shards(
    images, out_grad, conv_weight, proj_weight, gain_one, shift_one, gain_three, shift_three
):
    field = images[:, 0]
    cotangent = out_grad[:, 0]
    batch, depth, tile_rows, tile_cols = field.shape
    quadrants = lax.axis_size("sp")
    cell_count = float(quadrants * lax.axis_size("bn") * batch * tile_rows * tile_cols)
    per_image = 1.0 / float(quadrants * tile_rows * tile_cols)
    padded = extend(field)
    conv_out = conv_cells(padded, conv_weight, tile_rows, tile_cols)
    mean_one, var_one = group_moments(conv_out, cell_count)
    scale_one = lax.rsqrt(var_one + norm_floor)
    normed_one = (conv_out - channel(mean_one)) * channel(scale_one)
    before_act = channel(gain_one) * normed_one + channel(shift_one)
    hidden = jax.nn.silu(before_act).astype(jnp.bfloat16)
    widened = jnp.einsum("io,nihw->nohw", proj_weight, hidden, preferred_element_type=jnp.float32)
    mean_three, var_three = group_moments(widened, cell_count)
    scale_three = lax.rsqrt(var_three + norm_floor)
    normed_three = (widened - channel(mean_three)) * channel(scale_three)
    output_pre = channel(gain_three) * normed_three + channel(shift_three)
    grad_out = cotangent.astype(jnp.float32) * silu_slope(output_pre)
    grad_wide, sum_three, cross_three, group_sum_three, group_cross_three = norm_backward(
        grad_out, normed_three, gain_three, scale_three, cell_count
    )
    grad_proj = jnp.einsum("nihw,nohw->io", hidden, grad_wide, preferred_element_type=jnp.float32)
    grad_hidden = jnp.einsum(
        "io,nohw->nihw", proj_weight, grad_wide, preferred_element_type=jnp.float32
    )
    grad_pre = grad_hidden * silu_slope(before_act)
    grad_conv_out, sum_one, cross_one, group_sum_one, group_cross_one = norm_backward(
        grad_pre, normed_one, gain_one, scale_one, cell_count
    )
    grad_kernel = kernel_grad(padded, grad_conv_out, tile_rows, tile_cols)
    back_pad = extend(grad_conv_out)
    grad_field = conv_back(back_pad, conv_weight, tile_rows, tile_cols).astype(jnp.bfloat16)
    kernel_total, full_proj, cross_one, sum_one, cross_three, sum_three = lax.psum(
        (grad_kernel, grad_proj, cross_one, sum_one, cross_three, sum_three), ("sp", "bn", "dp")
    )
    return (
        grad_field[:, None],
        kernel_total * per_image,
        full_proj * per_image,
        cross_one * per_image,
        sum_one * per_image,
        cross_three * per_image,
        sum_three * per_image,
    )


def solution(mesh):
    in_specs = (
        P(("bn", "dp"), "sp", None, None, None),
        P(("bn", "dp"), "sp", None, None, None),
        P(),
        P(),
        P(),
        P(),
        P(),
        P(),
    )
    out_specs = (P(("bn", "dp"), "sp", None, None, None), P(), P(), P(), P(), P(), P())
    return jax.shard_map(shards, mesh=mesh, in_specs=in_specs, out_specs=out_specs, check_vma=False)
```

profile of v0, /device:TPU:0, one launch (start us, length us, event | category | flops | bytes accessed | tf_op | source)
XLA Modules:
  0.0 334.8 jit_solution(14096752386717749540)
XLA Ops:
  9.1 3.1 collective-permute-start
  12.2 1.7 collective-permute-done
  15.4 3.0 collective-permute-start.1
  18.4 3.9 %copy.36 = bf16[1,1,256,40,128]{2,4,3,1,0:T(8,128)(2,1)S(1)} copy(bf16[1,1,256,40,128]{4,3,2,1,0:T(8,128)(2,1)} %param.13) | data formatting | bytes 5242880 | tf_op args[1]
  23.7 3.1 pad_maximum_fusion
  34.7 19.4 %all-reduce.6 = (f32[512]{0:T(512)S(1)}, f32[512]{0:T(512)S(1)}) all-reduce(f32[512]{0:T(512)S(1)} %get-tuple-element.462, f32[512]{0:T(512)S(1)} %dynamic-update-slice.1), channel_id=2, replica_groups=mesh['sp'=4,'bn'=2,'dp'=4] {'sp','bn'}, use_global_device_ids=true, to_apply=%add | all-reduce | flops 1024 | bytes 8192
  54.7 2.8 fusion.115
  58.4 1.5 copy-done.1
  59.9 16.3 %all-gather.5 = f32[8,1,256]{2,1,0:T(1,128)S(1)} all-gather(f32[1,1,256]{2,1,0:T(1,128)S(1)} %bitcast.399), channel_id=5, replica_groups=mesh['sp'=4,'bn'=2,'dp'=4] {'sp','bn'}, dimensions={0}, use_global_device_ids=true | all-gather | bytes 9216 | tf_op jit(solution)/shard_map/all_gather | solution.py:14
  76.2 18.3 %all-gather.4 = f32[8,1,256]{2,1,0:T(1,128)S(1)} all-gather(f32[1,1,256]{2,1,0:T(1,128)S(1)} %bitcast.398), channel_id=4, replica_groups=mesh['sp'=4,'bn'=2,'dp'=4] {'sp','bn'}, dimensions={0}, use_global_device_ids=true | all-gather | bytes 9216 | tf_op jit(solution)/shard_map/all_gather | solution.py:14
  95.0 4.7 %fusion.111 = (f32[256]{0:T(256)S(1)}, f32[256]{0:T(256)S(1)}) fusion(f32[256]{0:T(256)S(1)} %copy-done.20, f32[256]{0:T(256)S(1)} %get-tuple-element.458, f32[256]{0:T(256)S(1)} %get-tuple-element.342, f32[40,128,256]{2,1,0:T(8,128)} %copy-done.1, f32[256]{0:T(256)S(1)} %copy-done.19, bf16[1,1,256,40,128]{2,4,3,1,0:T(8,128)(2,1)S(1)} %copy.36), kind=kLoop, calls=%fused_computation.206 | loop fusion | flops 20971008 | bytes 7870464 | tf_op jit(solution)/shard_map/reduce_sum | solution.py:122
  99.7 17.3 %all-reduce.5 = (f32[256]{0:T(256)S(1)}, f32[256]{0:T(256)S(1)}) all-reduce(f32[256]{0:T(256)S(1)} %get-tuple-element.400, f32[256]{0:T(256)S(1)} %get-tuple-element.399), channel_id=1, replica_groups=mesh['sp'=4,'bn'=2,'dp'=4] {'sp','bn'}, use_global_device_ids=true, to_apply=%region_11.12 | all-reduce | flops 512 | bytes 4096 | tf_op jit(solution)/shard_map/psum | solution.py:124
  117.0 5.3 %fusion.11 = bf16[256,40,128]{0,2,1:T(8,128)(2,1)S(1)} fusion(f32[40,128,256]{2,1,0:T(8,128)} %copy-done.1, f32[256]{0:T(256)S(1)} %get-tuple-element.435, f32[256]{0:T(256)S(1)} %broadcast_multiply_fusion.4, f32[256]{0:T(256)S(1)} %get-tuple-element.458, f32[256]{0:T(256)S(1)} %get-tuple-element.342, f32[256]{0:T(256)S(1)} %get-tuple-element.457, ...), kind=kLoop, calls=%fused_computation.29 | loop fusion | flops 24903680 | bytes 10492928 | tf_op jit(solution)/shard_map/reshape.42
  122.3 2.2 fusion.112
  124.6 1.3 convolution_bitcast_fusion.1
  125.8 38.3 %all-reduce.2 = (f32[64]{0:T(128)S(1)}, f32[64]{0:T(128)S(1)}, f32[256]{0:T(256)S(1)}, f32[256]{0:T(256)S(1)}) all-reduce(f32[64]{0:T(128)S(1)} %get-tuple-element.402, f32[64]{0:T(128)S(1)} %get-tuple-element.401, f32[256]{0:T(256)S(1)} %get-tuple-element.400, ...), channel_id=1, replica_groups=mesh['sp'=4,'bn'=2,'dp'=4] {'sp','bn','dp'}, use_global_device_ids=true, to_apply=%region_18.19 | all-reduce | flops 640 | bytes 5120 | tf_op jit(solution)/shard_map/psum | solution.py:167
  164.1 21.1 %all-reduce.4 = (f32[64]{0:T(128)S(1)}, f32[64]{0:T(128)S(1)}) all-reduce(f32[64]{0:T(128)S(1)} %get-tuple-element.402, f32[64]{0:T(128)S(1)} %get-tuple-element.401), channel_id=1, replica_groups=mesh['sp'=4,'bn'=2,'dp'=4] {'sp','bn'}, use_global_device_ids=true, to_apply=%region_15.16 | all-reduce | flops 128 | bytes 1024 | tf_op jit(solution)/shard_map/psum | solution.py:124
  185.2 1.8 fusion.19
  193.6 3.1 collective-permute-done.2
  198.0 4.3 %collective-permute-done.3 = bf16[1,64,1,130]{3,1,2,0:T(8,128)(2,1)S(1)} collective-permute-done((bf16[1,64,1,130]{3,1,2,0:T(8,128)(2,1)S(1)}, bf16[1,64,1,130]{3,1,2,0:T(8,128)(2,1)S(1)}, u32[]{:S(2)}, u32[]{:S(2)}) %collective-permute-start.3) | collective-permute-done | bytes 16672 | tf_op jit(solution)/shard_map/ppermute | solution.py:10
  202.3 1.8 maximum_maximum_fusion.1
  209.3 115.5 %all-reduce.9.cloned.1.call-done = (f32[3,3,64,64]{3,2,1,0:T(8,128)}, f32[64,256]{1,0:T(8,128)}) async-done(((f32[3,3,64,64]{3,2,1,0:T(8,128)}, f32[64,256]{1,0:T(8,128)}), (f32[3,3,64,64]{3,2,1,0:T(8,128)}, f32[64,256]{1,0:T(8,128)})) %all-reduce.9.cloned.1.call-update) | async-done | bytes 213008 | tf_op jit(solution)/shard_map/psum | solution.py:167
  324.8 1.7 broadcast_multiply_fusion
  326.5 1.5 broadcast_multiply_fusion.1
  (154 shorter events, 27.2 us)
Async XLA Ops:
  7.2 47.6 %copy-start = (bf16[64,256]{1,0:T(8,128)(2,1)S(1)}, bf16[64,256]{1,0:T(8,128)(2,1)}, u32[]{:S(2)}) copy-start(bf16[64,256]{1,0:T(8,128)(2,1)} %param.15) | copy-start | bytes 98308
  7.2 317.6 %all-reduce.9.cloned.1.call-start = ((), (), s32[]{:S(2)}) async-start(), calls=%async_computation | async-start | bytes 720896 | tf_op jit(solution)/shard_map/psum | solution.py:167
  9.1 4.7 %collective-permute-start = (bf16[1,64,40,1]{1,2,3,0:T(8,128)(2,1)S(1)}, bf16[1,64,40,1]{1,2,3,0:T(8,128)(2,1)S(1)}, u32[]{:S(2)}, u32[]{:S(2)}) collective-permute-start(bf16[1,64,40,1]{1,2,3,0:T(8,128)(2,1)S(1)} %copy.32), channel_id=1, source_target_pairs={{0,8},{8,0},{16,24},{24,16},{1,9},{9,1},{17,25},{25,17},{2,10},{10... | collective-permute-start | bytes 15368 | tf_op jit(solution)/shard_map/ppermute | solution.py:10
  15.4 8.2 %collective-permute-start.1 = (bf16[1,64,1,130]{3,1,2,0:T(8,128)(2,1)S(1)}, bf16[1,64,1,130]{3,1,2,0:T(8,128)(2,1)S(1)}, u32[]{:S(2)}, u32[]{:S(2)}) collective-permute-start(bf16[1,64,1,130]{3,1,2,0:T(8,128)(2,1)S(1)} %fusion.63), channel_id=1, source_target_pairs={{0,16},{8,24},{16,0},{24,8},{1,17},{9,25},{17,1},{25,9},{2,18},{10... | collective-permute-start | bytes 49928 | tf_op jit(solution)/shard_map/ppermute | solution.py:10
  18.4 3.9 %copy-start.23 = (u32[32]{0:T(128)S(1)}, u32[32]{0:T(128)}, u32[]{:S(2)}) copy-start(u32[32]{0:T(128)} %constant.150) | copy-start | bytes 388
  23.7 3.1 copy-start.17
  26.8 5.7 %copy-start.11 = (bf16[1,64,41,130]{3,1,2,0:T(8,128)(2,1)}, bf16[1,64,41,130]{3,1,2,0:T(8,128)(2,1)S(1)}, u32[]{:S(2)}) copy-start(bf16[1,64,41,130]{3,1,2,0:T(8,128)(2,1)S(1)} %get-tuple-element.447) | copy-start | bytes 2046724
  27.9 1.1 copy-start.6
  33.0 1.2 copy-start.8
  33.0 21.7 %copy-start.21 = (f32[64]{0:T(128)S(1)}, f32[64]{0:T(128)}, u32[]{:S(2)}) copy-start(f32[64]{0:T(128)} %param.16) | copy-start | bytes 772
  33.0 21.7 %copy-start.22 = (f32[64]{0:T(128)S(1)}, f32[64]{0:T(128)}, u32[]{:S(2)}) copy-start(f32[64]{0:T(128)} %param.17) | copy-start | bytes 772
  57.6 2.3 copy-start.1
  57.6 37.4 %copy-start.19 = (f32[256]{0:T(256)S(1)}, f32[256]{0:T(256)}, u32[]{:S(2)}) copy-start(f32[256]{0:T(256)} %param.18) | copy-start | bytes 3076
  57.6 37.4 %copy-start.20 = (f32[256]{0:T(256)S(1)}, f32[256]{0:T(256)}, u32[]{:S(2)}) copy-start(f32[256]{0:T(256)} %param.19) | copy-start | bytes 3076
  117.0 5.3 %copy-start.9 = (f32[40,128,64]{1,2,0:T(8,128)S(1)}, f32[40,128,64]{1,2,0:T(8,128)}, u32[]{:S(2)}) copy-start(f32[40,128,64]{1,2,0:T(8,128)} %copy-done.8) | copy-start | bytes 3932164
  124.5 60.7 %copy-start.10 = (f32[40,128,64]{1,2,0:T(8,128)S(1)}, f32[40,128,64]{1,2,0:T(8,128)}, u32[]{:S(2)}) copy-start(f32[40,128,64]{1,2,0:T(8,128)} %copy-done.8) | copy-start | bytes 3932164
  185.2 1.9 copy-start.14
  187.7 1.1 copy-start.7
  188.8 1.1 copy-start.16
  188.8 1.4 copy-start.4
  190.2 1.3 copy-start.12
  192.7 4.6 %copy-start.18 = (f32[9,64,64]{2,1,0:T(8,128)}, f32[9,64,64]{2,1,0:T(8,128)S(1)}, u32[]{:S(2)}) copy-start(f32[9,64,64]{2,1,0:T(8,128)S(1)} %fusion.24) | copy-start | bytes 442372
  193.0 3.7 %collective-permute-start.2 = (bf16[1,64,40,1]{1,2,3,0:T(8,128)(2,1)S(1)}, bf16[1,64,40,1]{1,2,3,0:T(8,128)(2,1)S(1)}, u32[]{:S(2)}, u32[]{:S(2)}) collective-permute-start(bf16[1,64,40,1]{1,2,3,0:T(8,128)(2,1)S(1)} %copy.38), channel_id=1, source_target_pairs={{0,8},{8,0},{16,24},{24,16},{1,9},{9,1},{17,25},{25,17},{2,10},{10... | collective-permute-start | bytes 15368 | tf_op jit(solution)/shard_map/ppermute | solution.py:10
  197.4 4.9 %collective-permute-start.3 = (bf16[1,64,1,130]{3,1,2,0:T(8,128)(2,1)S(1)}, bf16[1,64,1,130]{3,1,2,0:T(8,128)(2,1)S(1)}, u32[]{:S(2)}, u32[]{:S(2)}) collective-permute-start(bf16[1,64,1,130]{3,1,2,0:T(8,128)(2,1)S(1)} %fusion.62), channel_id=1, source_target_pairs={{0,16},{8,24},{16,0},{24,8},{1,17},{9,25},{17,1},{25,9},{2,18},{10... | collective-permute-start | bytes 49928 | tf_op jit(solution)/shard_map/ppermute | solution.py:10
  (5 other events, 5.1 us)
Sparse Core Ops, SparseCore 0:
  198.1 126.6 all-reduce.8
where the time goes:
time: 336 us; the launch traced here: 335 us
  blocking collectives  131 us (39%)
  waiting for transfers between devices  125 us (37%)
  other arithmetic  23.6 us (7%)
  matrix products  17.7 us (5%)
  local copies, waits for them, and re-layouts  16.4 us (5%)
  between operations  15.3 us (5%)
  starting transfers between devices  6.27 us (2%)
    psum x1, waiting for transfers between devices, shards(): lax.psum((grad_kernel, grad_proj, cross_one, sum_one, cross_three, sum_th...  116 us
    psum x2, blocking collectives, norm_backward(): group_sum, group_cross = lax.psum((local_sum, local_cross), ('sp', 'bn'))  38.4 us
    psum x1, blocking collectives, shards(): lax.psum((grad_kernel, grad_proj, cross_one, sum_one, cross_three, sum_th...  38.3 us
    all_gather x2, blocking collectives, combined_all(): everything = jax.tree.map(lambda part: lax.all_gather(part, axis), value)  34.6 us
    unnamed x1, blocking collectives  19.4 us
    unnamed x57, local copies, waits for them, and re-layouts  14.7 us
    ppermute x4, waiting for transfers between devices, from_partner(): lax.ppermute(value, axis, [(i, i ^ 1 << distance) for i in range(lax.axis...  9 us
  transfers between devices with their start and end apart: 5, of which 4 were waited for; matrix products, arithmetic and copies ran while one was open for 4% of the time, Pallas kernels for 0%

commit v1 on v0

v1 whole, which is shorter than its diff:
```python
import functools

import jax
import jax.numpy as jnp
from jax import lax
from jax.experimental import pallas as pl
from jax.experimental.pallas import tpu as pltpu
from jax.sharding import PartitionSpec as P

norm_floor = 1e-05
F32 = jnp.float32
BF16 = jnp.bfloat16
MESH = pl.DeviceIdType.MESH
LANES = 128
NT = (((1,), (1,)), ((), ()))


def sig(v):
    return 0.5 * jnp.tanh(0.5 * v) + 0.5


def to_row(col):
    return jnp.broadcast_to(col, (col.shape[0], LANES)).T[0:1]


def to_col(row):
    return jnp.broadcast_to(row, (LANES, row.shape[1])).T


def pick(count, options):
    return next(o for o in options if count % o == 0)


def kernel(
    n_sp, n_bn, n_dp,
    x_ref, g_ref, wf_ref, wb_ref, wpt_ref, wp_ref, vec1_ref, vec3_ref,
    ig_ref, cg_out, pg_out, q1_out, s1_out, q3_out, s3_out,
    xs, ds, a_buf, e1_buf, b_buf, e3_buf, y_buf, acc, cgt, gpt,
    packed, halo, stats, rs_send, rs_recv, line, fin,
    h_send, h_recv, st_send, st_recv, rs_ss, rs_rs, ln_ss, ln_rs, ag_ss, ag_rs,
):
    th, c, tw = x_ref.shape
    co = g_ref.shape[1]
    n_grp = n_sp * n_bn
    n_pl = n_bn * n_dp
    shard = line.shape[1]
    local_cells = float(th * tw)
    cells = local_cells * n_grp
    factor = 1.0 / (n_sp * local_cells)
    sp = lax.axis_index("sp")
    bn = lax.axis_index("bn")
    dp = lax.axis_index("dp")
    col = sp % 2
    rh = sp // 2
    me_g = sp * n_bn + bn
    me_p = bn * n_dp + dp

    def group_peer(d):
        p = (me_g + d) % n_grp
        return {"sp": p // n_bn, "bn": p % n_bn, "dp": dp}

    def plane_peer(d):
        p = (me_p + d) % n_pl
        return p, {"sp": sp, "bn": p // n_dp, "dp": p % n_dp}

    def line_peer(d):
        return {"sp": (sp + d) % n_sp, "bn": bn, "dp": dp}

    barrier = pltpu.get_barrier_semaphore()

    def greet_group(d, carry):
        pl.semaphore_signal(barrier, inc=1, device_id=group_peer(d), device_id_type=MESH)
        return carry

    def greet_plane(d, carry):
        pl.semaphore_signal(barrier, inc=1, device_id=plane_peer(d)[1], device_id_type=MESH)
        return carry

    lax.fori_loop(1, n_grp, greet_group, 0)
    lax.fori_loop(1, n_pl, greet_plane, 0)

    lane = lax.broadcasted_iota(jnp.int32, (c, tw), 1)
    left = lane == 0
    right = lane == tw - 1
    edge = (tw - 1) * (1 - col)
    edge_row = (1 - rh) * (th - 1)
    is_c1 = col.astype(F32)
    is_c0 = 1.0 - is_c1

    def pack_cols(get):
        def step(h, got):
            turned = pltpu.roll(get(h), (h + tw - edge) % tw, 1)
            return jnp.where(lane == h, turned, got)

        return lax.fori_loop(0, th, step, jnp.zeros((c, tw), F32))

    def halo_copies(k, row_src):
        out = []
        for s, (src, flip) in enumerate(((packed.at[k], 1), (row_src, 2), (row_src, 3))):
            pcol = col if flip == 2 else 1 - col
            prow = rh if flip == 1 else 1 - rh
            out.append(
                pltpu.make_async_remote_copy(
                    src_ref=src, dst_ref=halo.at[k, s], send_sem=h_send.at[k, s], recv_sem=h_recv.at[k, s],
                    device_id={"sp": prow * 2 + pcol, "bn": bn, "dp": dp}, device_id_type=MESH,
                )
            )
        return out

    def fill(dst, k, get):
        got = halo[k, 0].astype(F32)

        def step(h, carry):
            v = get(h)
            edge_col = pltpu.roll(got, (edge + tw - h) % tw, 1)
            dst[h + 1, 0:c] = jnp.where(left, edge_col * is_c1, pltpu.roll(v, 1, 1)).astype(BF16)
            dst[h + 1, c : 2 * c] = v.astype(BF16)
            dst[h + 1, 2 * c : 3 * c] = jnp.where(right, edge_col * is_c0, pltpu.roll(v, tw - 1, 1)).astype(BF16)
            return carry

        lax.fori_loop(0, th, step, 0)
        v = halo[k, 1].astype(F32)
        diag = halo[k, 2].astype(F32)
        real = (1 - rh) * (th + 1)
        dst[real, 0:c] = jnp.where(left, pltpu.roll(diag, 1, 1) * is_c1, pltpu.roll(v, 1, 1)).astype(BF16)
        dst[real, c : 2 * c] = v.astype(BF16)
        dst[real, 2 * c : 3 * c] = jnp.where(
            right, pltpu.roll(diag, tw - 1, 1) * is_c0, pltpu.roll(v, tw - 1, 1)
        ).astype(BF16)
        dst[rh * (th + 1)] = jnp.zeros((3 * c, tw), BF16)

    def exchange(k, first, second):
        n = first.shape[1]
        stats[k, me_g, 0:1, 0:n] = first
        stats[k, me_g, 1:2, 0:n] = second

        def copy_to(d):
            return pltpu.make_async_remote_copy(
                src_ref=stats.at[k, me_g], dst_ref=stats.at[k, me_g],
                send_sem=st_send.at[k, d], recv_sem=st_recv.at[k, d],
                device_id=group_peer(d), device_id_type=MESH,
            )

        def start(d, carry):
            copy_to(d).start()
            return carry

        def finish(d, carry):
            src = (me_g + n_grp - d) % n_grp
            arrival = pltpu.make_async_remote_copy(
                src_ref=stats.at[k, me_g], dst_ref=stats.at[k, src],
                send_sem=st_send.at[k, d], recv_sem=st_recv.at[k, d],
                device_id=group_peer(d), device_id_type=MESH,
            )
            arrival.wait_recv()
            arrival.wait_send()
            return carry

        lax.fori_loop(1, n_grp, start, 0)
        lax.fori_loop(1, n_grp, finish, 0)
        firsts = [stats[k, j, 0:1, 0:n] for j in range(n_grp)]
        seconds = [stats[k, j, 1:2, 0:n] for j in range(n_grp)]
        return firsts, seconds

    def moments(k, mean_row, square_row):
        means, squares = exchange(k, mean_row, square_row)
        mean = sum(means[1:], means[0]) / float(n_grp)
        square = sum(squares[1:], squares[0])
        for m in means:
            square = square + local_cells * (m - mean) * (m - mean)
        return mean, square / cells

    def sums(k, first, second):
        a, b = exchange(k, first, second)
        return sum(a[1:], a[0]), sum(b[1:], b[0])

    def row_sum(v):
        return jnp.sum(v.T, axis=0, keepdims=True)

    get_x = lambda h: x_ref[h].astype(F32)
    packed[0] = pack_cols(get_x).astype(BF16)
    pl.semaphore_wait(barrier, n_grp - 1 + n_pl - 1)
    x_copies = halo_copies(0, x_ref.at[edge_row])
    for copy in x_copies:
        copy.start()
    for copy in x_copies:
        copy.wait()
    fill(xs, 0, get_x)

    r4 = pick(th, (4, 2, 1))
    r8 = pick(th, (8, 4, 2, 1))
    r2 = pick(th, (2, 1))

    def columns(src, h, r):
        return jnp.concatenate([src[pl.ds(h + k, 3)].reshape(9 * c, tw) for k in range(r)], axis=1)

    def conv_step(t, got):
        h = t * r4
        res = jnp.dot(wf_ref[...], columns(xs, h, r4), preferred_element_type=F32)
        for k in range(r4):
            piece = res[:, k * tw : (k + 1) * tw]
            a_buf[h + k] = piece
            got = got + piece
        return got

    zero_c = jnp.zeros((c, tw), F32)
    total = lax.fori_loop(0, th // r4, conv_step, zero_c)
    mean_col = jnp.sum(total, axis=1, keepdims=True) / local_cells

    def square_step(h, got):
        d = a_buf[h] - mean_col
        return got + d * d

    sq = lax.fori_loop(0, th, square_step, zero_c)
    mu1, var1 = moments(0, to_row(mean_col), row_sum(sq))
    s1 = lax.rsqrt(var1 + norm_floor)
    gain1 = vec1_ref[0:1]
    mu1_c = to_col(mu1)
    s1_c = to_col(s1)
    gain1_c = to_col(gain1)
    shift1_c = to_col(vec1_ref[1:2])

    acc[...] = jnp.zeros_like(acc)

    def wide_step(t, carry):
        h = t * r2
        parts = []
        for k in range(r2):
            n1 = (a_buf[h + k] - mu1_c) * s1_c
            a_buf[h + k] = n1
            p1 = gain1_c * n1 + shift1_c
            parts.append((p1 * sig(p1)).astype(BF16))
        y = jnp.concatenate(parts, axis=1)
        y_buf[:, pl.ds(pl.multiple_of(h * tw, tw), r2 * tw)] = y
        res = jnp.dot(wpt_ref[...], y, preferred_element_type=F32)
        more = None
        for k in range(r2):
            piece = res[:, k * tw : (k + 1) * tw]
            b_buf[h + k] = piece
            more = piece if more is None else more + piece
        acc[...] += more
        return carry

    lax.fori_loop(0, th // r2, wide_step, 0)
    mean3_col = jnp.sum(acc[...], axis=1, keepdims=True) / local_cells
    sq_rows = []
    for j in range(0, co, c):
        m = jnp.broadcast_to(mean3_col[j : j + c], (c, tw))

        def square3(h, got, j=j, m=m):
            d = b_buf[h, j : j + c] - m
            return got + d * d

        sq_rows.append(row_sum(lax.fori_loop(0, th, square3, zero_c, unroll=2)))
    mu3, var3 = moments(1, to_row(mean3_col), jnp.concatenate(sq_rows, axis=1))
    s3 = lax.rsqrt(var3 + norm_floor)
    gain3 = vec3_ref[0:1]
    mu3_c = to_col(mu3)
    s3_c = to_col(s3)
    gain3_c = to_col(gain3)
    shift3_c = to_col(vec3_ref[1:2])

    sum_rows, cross_rows = [], []
    for j in range(0, co, c):
        mu_j = mu3_c[j : j + c]
        s_j = s3_c[j : j + c]
        g_j = gain3_c[j : j + c]
        b_j = shift3_c[j : j + c]

        def out_step(h, got, j=j, mu_j=mu_j, s_j=s_j, g_j=g_j, b_j=b_j):
            n3 = (b_buf[h, j : j + c] - mu_j) * s_j
            p3 = g_j * n3 + b_j
            g = sig(p3)
            e3 = g_ref[h, j : j + c].astype(F32) * (g * (1.0 + p3 * (1.0 - g)))
            b_buf[h, j : j + c] = n3
            e3_buf[h, j : j + c] = e3
            return got[0] + e3, got[1] + e3 * n3

        ssum, scross = lax.fori_loop(0, th, out_step, (zero_c, zero_c))
        sum_rows.append(row_sum(ssum))
        cross_rows.append(row_sum(scross))
    local_s3 = jnp.concatenate(sum_rows, axis=1)
    local_q3 = jnp.concatenate(cross_rows, axis=1)
    full_s3, full_q3 = sums(2, local_s3, local_q3)
    coef_a = to_col(gain3 * s3)
    coef_s = to_col(full_s3 / cells)
    coef_q = to_col(full_q3 / cells)

    gpt[...] = jnp.zeros_like(gpt)

    def back_step(t, got):
        h = t * r2
        parts = []
        for k in range(r2):
            pieces = []
            for j in range(0, co, c):
                q = slice(j, j + c)
                db = coef_a[q] * (e3_buf[h + k, q] - coef_s[q] - b_buf[h + k, q] * coef_q[q])
                pieces.append(db.astype(BF16))
            parts.append(jnp.concatenate(pieces, axis=0))
        db = jnp.concatenate(parts, axis=1)
        y = y_buf[:, pl.ds(pl.multiple_of(h * tw, tw), r2 * tw)]
        gpt[...] += lax.dot_general(db, y, NT, preferred_element_type=F32)
        gh = jnp.dot(wp_ref[...], db, preferred_element_type=F32)
        ssum, scross = got
        for k in range(r2):
            n1 = a_buf[h + k]
            p1 = gain1_c * n1 + shift1_c
            g = sig(p1)
            e1 = gh[:, k * tw : (k + 1) * tw] * (g * (1.0 + p1 * (1.0 - g)))
            e1_buf[h + k] = e1
            ssum = ssum + e1
            scross = scross + e1 * n1
        return ssum, scross

    ssum, scross = lax.fori_loop(0, th // r2, back_step, (zero_c, zero_c))
    local_s1 = row_sum(ssum)
    local_q1 = row_sum(scross)
    full_s1, full_q1 = sums(3, local_s1, local_q1)
    d_a = to_col(gain1 * s1)
    d_s = to_col(full_s1 / cells)
    d_q = to_col(full_q1 / cells)

    def da_step(h, got):
        da = (d_a * (e1_buf[h] - d_s - a_buf[h] * d_q)).astype(BF16)
        ds[h + 1, c : 2 * c] = da
        turned = pltpu.roll(da.astype(F32), (h + tw - edge) % tw, 1)
        return jnp.where(lane == h, turned, got)

    packed[1] = lax.fori_loop(0, th, da_step, zero_c).astype(BF16)
    d_copies = halo_copies(1, ds.at[edge_row + 1, pl.ds(c, c)])
    for copy in d_copies:
        copy.start()

    cgt[...] = jnp.zeros_like(cgt)

    def grad_step(t, carry):
        h = t * r8
        da = jnp.concatenate([ds[h + k + 1, c : 2 * c] for k in range(r8)], axis=1)
        cgt[...] += lax.dot_general(columns(xs, h, r8), da, NT, preferred_element_type=F32)
        return carry

    lax.fori_loop(0, th // r8, grad_step, 0)
    half = 9 * c // 2
    flat = jnp.concatenate([cgt[k * c : (k + 1) * c, :].T for k in range(9)], axis=0)
    rs_send[0:half] = jnp.concatenate([flat[:half], flat[half:]], axis=1)
    gp = gpt[...].T
    base = half
    for k in range(co // LANES):
        rs_send[base : base + c] = gp[:, k * LANES : (k + 1) * LANES]
        base += c
    rs_send[base:] = jnp.zeros((rs_send.shape[0] - base, LANES), F32)
    rs_send[base : base + 1] = jnp.concatenate([local_q1, local_s1], axis=1)
    small = base + 1
    for v in (local_q3, local_s3):
        for k in range(co // LANES):
            rs_send[small : small + 1] = v[:, k * LANES : (k + 1) * LANES]
            small += 1

    def span(p):
        return pl.ds(pl.multiple_of(p * shard, 8), shard)

    def rs_copy(d):
        p, where = plane_peer(d)
        return pltpu.make_async_remote_copy(
            src_ref=rs_send.at[span(p)], dst_ref=rs_recv.at[d], send_sem=rs_ss.at[d], recv_sem=rs_rs.at[d],
            device_id=where, device_id_type=MESH,
        )

    def rs_start(d, carry):
        rs_copy(d).start()
        return carry

    lax.fori_loop(1, n_pl, rs_start, 0)
    for copy in d_copies:
        copy.wait()

    fill(ds, 1, lambda h: ds[h + 1, c : 2 * c].astype(F32))

    def field_step(t, carry):
        h = t * r4
        res = jnp.dot(wb_ref[...], columns(ds, h, r4), preferred_element_type=F32)
        for k in range(r4):
            ig_ref[h + k] = res[:, k * tw : (k + 1) * tw].astype(BF16)
        return carry

    lax.fori_loop(0, th // r4, field_step, 0)

    def rs_wait(d, got):
        rs_copy(d).wait()
        return got + rs_recv[d]

    line[sp] = lax.fori_loop(1, n_pl, rs_wait, rs_send[span(me_p)])

    def ln_copy(d, slot):
        return pltpu.make_async_remote_copy(
            src_ref=line.at[sp], dst_ref=line.at[slot], send_sem=ln_ss.at[d], recv_sem=ln_rs.at[d],
            device_id=line_peer(d), device_id_type=MESH,
        )

    for d in range(1, n_sp):
        ln_copy(d, sp).start()
    for d in range(1, n_sp):
        ln_copy(d, (sp + n_sp - d) % n_sp).wait()
    whole = line[0]
    for k in range(1, n_sp):
        whole = whole + line[k]
    fin[span(me_p)] = whole * factor

    def ag_copy(d, slot):
        return pltpu.make_async_remote_copy(
            src_ref=fin.at[span(me_p)], dst_ref=fin.at[span(slot)], send_sem=ag_ss.at[d], recv_sem=ag_rs.at[d],
            device_id=plane_peer(d)[1], device_id_type=MESH,
        )

    def ag_start(d, carry):
        ag_copy(d, me_p).start()
        return carry

    def ag_wait(d, carry):
        ag_copy(d, (me_p + n_pl - d) % n_pl).wait()
        return carry

    lax.fori_loop(1, n_pl, ag_start, 0)
    lax.fori_loop(1, n_pl, ag_wait, 0)
    cg_out[0:half] = fin[0:half, 0:c]
    cg_out[half:] = fin[0:half, c : 2 * c]
    base = half
    for k in range(co // LANES):
        pg_out[:, k * LANES : (k + 1) * LANES] = fin[base : base + c]
        base += c
    q1_out[...] = fin[base : base + 1, 0:c]
    s1_out[...] = fin[base : base + 1, c : 2 * c]
    small = base + 1
    for ref in (q3_out, s3_out):
        for k in range(co // LANES):
            ref[:, k * LANES : (k + 1) * LANES] = fin[small : small + 1]
            small += 1


def shards(images, out_grad, conv_weight, proj_weight, gain_one, shift_one, gain_three, shift_three):
    _, _, c, th, tw = images.shape
    co = out_grad.shape[2]
    n_sp, n_bn, n_dp = (lax.axis_size(a) for a in ("sp", "bn", "dp"))
    n_grp, n_pl = n_sp * n_bn, n_bn * n_dp
    x = images[0, 0].transpose(1, 0, 2)
    g = out_grad[0, 0].transpose(1, 0, 2)
    wf = conv_weight.transpose(2, 0, 1, 3).reshape(c, 9 * c)
    wb = conv_weight[::-1, ::-1].transpose(3, 0, 1, 2).reshape(c, 9 * c)
    rows = 9 * c // 2 + c * (co // LANES) + 1 + 2 * (co // LANES)
    shard = 8 * (-(-rows // (8 * n_pl)))
    vm = pl.BlockSpec(memory_space=pltpu.VMEM)
    dma = pltpu.SemaphoreType.DMA
    outs = pl.pallas_call(
        functools.partial(kernel, n_sp, n_bn, n_dp),
        out_shape=(
            jax.ShapeDtypeStruct((th, c, tw), BF16),
            jax.ShapeDtypeStruct((9 * c, c), F32),
            jax.ShapeDtypeStruct((c, co), F32),
            jax.ShapeDtypeStruct((1, c), F32),
            jax.ShapeDtypeStruct((1, c), F32),
            jax.ShapeDtypeStruct((1, co), F32),
            jax.ShapeDtypeStruct((1, co), F32),
        ),
        in_specs=[vm] * 8,
        out_specs=(vm,) * 7,
        scratch_shapes=[
            pltpu.VMEM((th + 2, 3 * c, tw), BF16),
            pltpu.VMEM((th + 2, 3 * c, tw), BF16),
            pltpu.VMEM((th, c, tw), F32),
            pltpu.VMEM((th, c, tw), F32),
            pltpu.VMEM((th, co, tw), F32),
            pltpu.VMEM((th, co, tw), F32),
            pltpu.VMEM((c, th * tw), BF16),
            pltpu.VMEM((co, tw), F32),
            pltpu.VMEM((9 * c, c), F32),
            pltpu.VMEM((co, c), F32),
            pltpu.VMEM((2, c, tw), BF16),
            pltpu.VMEM((2, 3, c, tw), BF16),
            pltpu.VMEM((4, n_grp, 8, co), F32),
            pltpu.VMEM((n_pl * shard, LANES), F32),
            pltpu.VMEM((n_pl, shard, LANES), F32),
            pltpu.VMEM((n_sp, shard, LANES), F32),
            pltpu.VMEM((n_pl * shard, LANES), F32),
            dma((2, 3)), dma((2, 3)),
            dma((4, n_grp)), dma((4, n_grp)),
            dma((n_pl,)), dma((n_pl,)),
            dma((n_sp,)), dma((n_sp,)),
            dma((n_pl,)), dma((n_pl,)),
        ],
        compiler_params=pltpu.CompilerParams(
            collective_id=0, has_side_effects=True, vmem_limit_bytes=60 * 1024 * 1024
        ),
        name="branch_step",
    )(
        x, g, wf, wb, proj_weight.T, proj_weight,
        jnp.stack([gain_one, shift_one]), jnp.stack([gain_three, shift_three]),
    )
    ig, cg, pg, q1, s1, q3, s3 = outs
    return (
        ig.transpose(1, 0, 2)[None, None],
        cg.reshape(conv_weight.shape),
        pg, q1[0], s1[0], q3[0], s3[0],
    )


def solution(mesh):
    tiles = P(("bn", "dp"), "sp", None, None, None)
    return jax.shard_map(
        shards,
        mesh=mesh,
        in_specs=(tiles, tiles) + (P(),) * 6,
        out_specs=(tiles,) + (P(),) * 6,
        check_vma=False,
    )
```

time: 336 us -> 99.4 us (0.30)
  blocking collectives: 131 us -> 0 us
  waiting for transfers between devices: 125 us -> 0 us
  Pallas kernels: 0 us -> 74.5 us
  other arithmetic: 23.6 us -> 2.53 us
  matrix products: 17.7 us -> 0 us
  between operations: 15.3 us -> 0.65 us
  starting transfers between devices: 6.27 us -> 0 us
  local copies, waits for them, and re-layouts: 16.4 us -> 21.2 us
    psum x1 -> x0, waiting for transfers between devices: 116 us -> none  [shards(): lax.psum((grad_kernel, grad_proj, cross_one, sum_one, cross_three, sum_th...]
    psum x3 -> x0, blocking collectives: 76.7 us -> none  [the longest x2 38.4 us: norm_backward(): group_sum, group_cross = lax.psum((local_sum, local_cross), ('sp', 'bn'))]
    pallas_call x0 -> x1, Pallas kernels: none -> 74.5 us  [shards(): pl.pallas_call(functools.partial(kernel, n_sp, n_bn, n_dp), out_shape=(ja...]
    all_gather x2 -> x0, blocking collectives: 34.6 us -> none  [combined_all(): everything = jax.tree.map(lambda part: lax.all_gather(part, axis), value)]
    unnamed x1 -> x0, blocking collectives: 19.4 us -> none
    dot_general x30 -> x0, matrix products: 17.7 us -> none  [the longest x9 3.89 us: conv_back(): jnp.einsum('oi,nohw->nihw', kernel[row_off, col_off], window, preferred_e...]
    ppermute x4 -> x0, waiting for transfers between devices: 9 us -> none  [from_partner(): lax.ppermute(value, axis, [(i, i ^ 1 << distance) for i in range(lax.axis...]
    ppermute x4 -> x0, starting transfers between devices: 6.24 us -> none  [from_partner(): lax.ppermute(value, axis, [(i, i ^ 1 << distance) for i in range(lax.axis...]
  transfers between devices with their start and end apart: 5 -> 0, of which waited for: 4 -> 0; matrix products, arithmetic and copies ran while one was open for 4% -> 0% of each run, Pallas kernels for 0% -> 0%
where the time goes in v1:
time: 99.4 us; the launch traced here: 98.9 us
  Pallas kernels  74.5 us (75%)
  local copies, waits for them, and re-layouts  21.2 us (21%)
  other arithmetic  2.53 us (3%)
    pallas_call x1, Pallas kernels, shards(): pl.pallas_call(functools.partial(kernel, n_sp, n_bn, n_dp), out_shape=(ja...  74.5 us
    unnamed x10, local copies, waits for them, and re-layouts  17.7 us

profile of v1, /device:TPU:0, one launch (start us, length us, event | category | flops | bytes accessed | tf_op | source)
XLA Modules:
  0.0 98.9 jit_solution(2362228943459292189)
XLA Ops:
  0.6 1.2 %pad_maximum_fusion.1.vec1_ref = f32[2,64]{1,0:T(2,128)} fusion(f32[1,64]{1,0:T(1,128)} %bitcast.40, f32[1,64]{1,0:T(1,128)} %bitcast.41), kind=kLoop, calls=%fused_computation.3 | loop fusion | flops 128 | bytes 1024 | tf_op jit(solution)/shard_map/stack | solution.py:497
  1.9 1.3 %pad_maximum_fusion.vec3_ref = f32[2,256]{1,0:T(2,128)} fusion(f32[1,256]{1,0:T(1,128)} %bitcast.38, f32[1,256]{1,0:T(1,128)} %bitcast.39), kind=kLoop, calls=%fused_computation.2 | loop fusion | flops 512 | bytes 4096 | tf_op jit(solution)/shard_map/stack | solution.py:497
  3.2 1.5 %copy.24 = bf16[64,256]{0,1:T(8,128)(2,1)} copy(bf16[64,256]{1,0:T(8,128)(2,1)} %wp_ref.1) | data formatting | bytes 65536 | tf_op args[3]
  4.7 1.0 %copy.23 = bf16[64,3,3,64]{0,3,2,1:T(8,128)(2,1)S(1)} copy(bf16[64,3,3,64]{3,0,2,1:T(8,128)(2,1)} %bitcast.31) | data formatting | bytes 147456 | tf_op jit(solution)/shard_map/transpose | solution.py:448
  5.7 0.8 copy.25.wf_ref
  6.5 0.9 rev.3
  7.4 0.8 copy.26.wb_ref
  8.2 2.1 %copy.31 = bf16[1,1,64,40,128]{4,2,3,1,0:T(8,128)(2,1)} copy(bf16[1,1,64,40,128]{4,3,2,1,0:T(8,128)(2,1)} %param.8) | data formatting | bytes 1310720 | tf_op args[0]
  10.2 3.9 %copy.30 = bf16[1,1,256,40,128]{4,2,3,1,0:T(8,128)(2,1)} copy(bf16[1,1,256,40,128]{4,3,2,1,0:T(8,128)(2,1)} %param.9) | data formatting | bytes 5242880 | tf_op args[1]
  14.1 74.5 %branch_step.1 = (bf16[40,64,128]{2,1,0:T(8,128)(2,1)}, f32[576,64]{1,0:T(8,128)}, f32[64,256]{1,0:T(8,128)}, f32[1,64]{1,0:T(1,128)}, f32[1,64]{1,0:T(1,128)}, /*index=5*/f32[1,256]{1,0:T(1,128)}, f32[1,256]{1,0:T(1,128)}) custom-call(bf16[40,64,128]{2,1,0:T(8,128)(2,1)} %bitcast.29, bf16[40,256,128]{2,1,0:T(8,128)(2,1)} %bitcast.28, ...), custom_call_target="tpu_custom_call" | custom-call | tf_op jit(solution)/shard_map/branch_step/pallas_call | solution.py:454
  88.7 2.4 %copy.27 = bf16[1,1,64,40,128]{4,3,2,1,0:T(8,128)(2,1)} copy(bf16[1,1,64,40,128]{4,2,3,1,0:T(8,128)(2,1)} %bitcast.30) | data formatting | bytes 1310720
  91.0 1.7 %copy.38 = f32[3,3,64,64]{3,2,1,0:T(8,128)} copy(f32[3,3,64,64]{3,2,1,0:T(8,128)} %bitcast.34) | data formatting | bytes 294912
  92.7 1.5 %copy.39 = f32[64,256]{1,0:T(8,128)} copy(f32[64,256]{1,0:T(8,128)} %get-tuple-element.44) | data formatting | bytes 131072
  94.2 1.1 %copy.40 = f32[64]{0:T(128)} copy(f32[64]{0:T(128)} %bitcast.43) | data formatting | bytes 512
  95.3 1.2 %copy.41 = f32[64]{0:T(128)} copy(f32[64]{0:T(128)} %bitcast.42) | data formatting | bytes 512
  96.5 1.2 %copy.42 = f32[256]{0:T(256)} copy(f32[256]{0:T(256)} %bitcast.37) | data formatting | bytes 2048
  97.7 1.2 %copy.43 = f32[256]{0:T(256)} copy(f32[256]{0:T(256)} %bitcast.36) | data formatting | bytes 2048

commit v2 on v1

--- a/solution.py
+++ b/solution.py
@@ -33,14 +33,15 @@
 
 def kernel(
     n_sp, n_bn, n_dp,
-    x_ref, g_ref, wf_ref, wb_ref, wpt_ref, wp_ref, vec1_ref, vec3_ref,
-    ig_ref, cg_out, pg_out, q1_out, s1_out, q3_out, s3_out,
+    x_hbm, g_hbm, cw_ref, wp_ref, gain1_ref, shift1_ref, gain3_ref, shift3_ref,
+    ig_ref, fin,
+    x_raw, g_raw, xf, gf, x_sem, g_sem, wf_ref, wb_ref, wpt_ref,
     xs, ds, a_buf, e1_buf, b_buf, e3_buf, y_buf, acc, cgt, gpt,
-    packed, halo, stats, rs_send, rs_recv, line, fin,
+    packed, edge_x, halo, stats, rs_send, rs_recv, line,
     h_send, h_recv, st_send, st_recv, rs_ss, rs_rs, ln_ss, ln_rs, ag_ss, ag_rs,
 ):
-    th, c, tw = x_ref.shape
-    co = g_ref.shape[1]
+    c, th, tw = x_raw.shape
+    co = g_raw.shape[0]
     n_grp = n_sp * n_bn
     n_pl = n_bn * n_dp
     shard = line.shape[1]
@@ -66,6 +67,11 @@
     def line_peer(d):
         return {"sp": (sp + d) % n_sp, "bn": bn, "dp": dp}
 
+    load_x = pltpu.make_async_copy(x_hbm, x_raw, x_sem)
+    load_g = pltpu.make_async_copy(g_hbm, g_raw, g_sem)
+    load_x.start()
+    load_g.start()
+
     barrier = pltpu.get_barrier_semaphore()
 
     def greet_group(d, carry):
@@ -129,7 +135,7 @@
         ).astype(BF16)
         dst[rh * (th + 1)] = jnp.zeros((3 * c, tw), BF16)
 
-    def exchange(k, first, second):
+    def exchange(k, first, second, meanwhile):
         n = first.shape[1]
         stats[k, me_g, 0:1, 0:n] = first
         stats[k, me_g, 1:2, 0:n] = second
@@ -157,32 +163,50 @@
             return carry
 
         lax.fori_loop(1, n_grp, start, 0)
+        meanwhile()
         lax.fori_loop(1, n_grp, finish, 0)
         firsts = [stats[k, j, 0:1, 0:n] for j in range(n_grp)]
         seconds = [stats[k, j, 1:2, 0:n] for j in range(n_grp)]
         return firsts, seconds
 
-    def moments(k, mean_row, square_row):
-        means, squares = exchange(k, mean_row, square_row)
+    def moments(k, mean_row, square_row, meanwhile):
+        means, squares = exchange(k, mean_row, square_row, meanwhile)
         mean = sum(means[1:], means[0]) / float(n_grp)
         square = sum(squares[1:], squares[0])
         for m in means:
             square = square + local_cells * (m - mean) * (m - mean)
         return mean, square / cells
 
-    def sums(k, first, second):
-        a, b = exchange(k, first, second)
+    def sums(k, first, second, meanwhile):
+        a, b = exchange(k, first, second, meanwhile)
         return sum(a[1:], a[0]), sum(b[1:], b[0])
 
     def row_sum(v):
         return jnp.sum(v.T, axis=0, keepdims=True)
 
-    get_x = lambda h: x_ref[h].astype(F32)
+    load_x.wait()
+
+    def widen(raw, out, block):
+        def step(j, carry):
+            rows = pl.ds(pl.multiple_of(j * block, block), block)
+            to = pl.ds(pl.multiple_of(j * block * th, 8), block * th)
+            out[to] = raw[rows].astype(F32).reshape(block * th, tw)
+            return carry
+
+        lax.fori_loop(0, raw.shape[0] // block, step, 0)
+
+    widen(x_raw, xf, 8)
+    get_x = lambda h: xf[pl.ds(h, c, stride=th), :]
     packed[0] = pack_cols(get_x).astype(BF16)
+    edge_x[...] = get_x(edge_row).astype(BF16)
     pl.semaphore_wait(barrier, n_grp - 1 + n_pl - 1)
-    x_copies = halo_copies(0, x_ref.at[edge_row])
+    x_copies = halo_copies(0, edge_x)
     for copy in x_copies:
         copy.start()
+    for k in range(9):
+        wf_ref[:, k * c : (k + 1) * c] = cw_ref[k]
+    load_g.wait()
+    widen(g_raw, gf, 8)
     for copy in x_copies:
         copy.wait()
     fill(xs, 0, get_x)
@@ -212,13 +236,20 @@
         return got + d * d
 
     sq = lax.fori_loop(0, th, square_step, zero_c)
-    mu1, var1 = moments(0, to_row(mean_col), row_sum(sq))
+    gain1 = gain1_ref[...]
+    gain3 = gain3_ref[...]
+
+    def prepare():
+        wpt_ref[...] = wp_ref[...].astype(F32).T.astype(BF16)
+        for k in range(9):
+            wb_ref[:, k * c : (k + 1) * c] = cw_ref[8 - k].astype(F32).T.astype(BF16)
+
+    mu1, var1 = moments(0, to_row(mean_col), row_sum(sq), prepare)
     s1 = lax.rsqrt(var1 + norm_floor)
-    gain1 = vec1_ref[0:1]
     mu1_c = to_col(mu1)
     s1_c = to_col(s1)
     gain1_c = to_col(gain1)
-    shift1_c = to_col(vec1_ref[1:2])
+    shift1_c = to_col(shift1_ref[...])
 
     acc[...] = jnp.zeros_like(acc)
 
@@ -252,13 +283,22 @@
             return got + d * d
 
         sq_rows.append(row_sum(lax.fori_loop(0, th, square3, zero_c, unroll=2)))
-    mu3, var3 = moments(1, to_row(mean3_col), jnp.concatenate(sq_rows, axis=1))
+
+    def slopes():
+        def step(h, carry):
+            p1 = gain1_c * a_buf[h] + shift1_c
+            g = sig(p1)
+            e1_buf[h] = g * (1.0 + p1 * (1.0 - g))
+            return carry
+
+        lax.fori_loop(0, th, step, 0)
+
+    mu3, var3 = moments(1, to_row(mean3_col), jnp.concatenate(sq_rows, axis=1), slopes)
     s3 = lax.rsqrt(var3 + norm_floor)
-    gain3 = vec3_ref[0:1]
     mu3_c = to_col(mu3)
     s3_c = to_col(s3)
     gain3_c = to_col(gain3)
-    shift3_c = to_col(vec3_ref[1:2])
+    shift3_c = to_col(shift3_ref[...])
 
     sum_rows, cross_rows = [], []
     for j in range(0, co, c):
@@ -271,7 +311,7 @@
             n3 = (b_buf[h, j : j + c] - mu_j) * s_j
             p3 = g_j * n3 + b_j
             g = sig(p3)
-            e3 = g_ref[h, j : j + c].astype(F32) * (g * (1.0 + p3 * (1.0 - g)))
+            e3 = gf[pl.ds(j * th + h, c, stride=th), :] * (g * (1.0 + p3 * (1.0 - g)))
             b_buf[h, j : j + c] = n3
             e3_buf[h, j : j + c] = e3
             return got[0] + e3, got[1] + e3 * n3
@@ -281,7 +321,7 @@
         cross_rows.append(row_sum(scross))
     local_s3 = jnp.concatenate(sum_rows, axis=1)
     local_q3 = jnp.concatenate(cross_rows, axis=1)
-    full_s3, full_q3 = sums(2, local_s3, local_q3)
+    full_s3, full_q3 = sums(2, local_s3, local_q3, lambda: None)
     coef_a = to_col(gain3 * s3)
     coef_s = to_col(full_s3 / cells)
     coef_q = to_col(full_q3 / cells)
@@ -305,9 +345,7 @@
         ssum, scross = got
         for k in range(r2):
             n1 = a_buf[h + k]
-            p1 = gain1_c * n1 + shift1_c
-            g = sig(p1)
-            e1 = gh[:, k * tw : (k + 1) * tw] * (g * (1.0 + p1 * (1.0 - g)))
+            e1 = gh[:, k * tw : (k + 1) * tw] * e1_buf[h + k]
             e1_buf[h + k] = e1
             ssum = ssum + e1
             scross = scross + e1 * n1
@@ -316,7 +354,7 @@
     ssum, scross = lax.fori_loop(0, th // r2, back_step, (zero_c, zero_c))
     local_s1 = row_sum(ssum)
     local_q1 = row_sum(scross)
-    full_s1, full_q1 = sums(3, local_s1, local_q1)
+    full_s1, full_q1 = sums(3, local_s1, local_q1, lambda: None)
     d_a = to_col(gain1 * s1)
     d_s = to_col(full_s1 / cells)
     d_q = to_col(full_q1 / cells)
@@ -384,7 +422,6 @@
             ig_ref[h + k] = res[:, k * tw : (k + 1) * tw].astype(BF16)
         return carry
 
-    lax.fori_loop(0, th // r4, field_step, 0)
 
     def rs_wait(d, got):
         rs_copy(d).wait()
@@ -400,6 +437,8 @@
 
     for d in range(1, n_sp):
         ln_copy(d, sp).start()
+    middle = th // r4 // 2
+    lax.fori_loop(0, middle, field_step, 0)
     for d in range(1, n_sp):
         ln_copy(d, (sp + n_sp - d) % n_sp).wait()
     whole = line[0]
@@ -422,7 +461,20 @@
         return carry
 
     lax.fori_loop(1, n_pl, ag_start, 0)
+    lax.fori_loop(middle, th // r4, field_step, 0)
     lax.fori_loop(1, n_pl, ag_wait, 0)
+
+
+def finish_kernel(ig_in, fin, ig_out, cg_out, pg_out, q1_out, s1_out, q3_out, s3_out, turned):
+    th, c, tw = ig_in.shape
+    co = pg_out.shape[1]
+
+    def step(h, carry):
+        turned[pl.ds(h, c, stride=th), :] = ig_in[h].astype(F32)
+        return carry
+
+    lax.fori_loop(0, th, step, 0)
+    half = 9 * c // 2
     cg_out[0:half] = fin[0:half, 0:c]
     cg_out[half:] = fin[0:half, c : 2 * c]
     base = half
@@ -437,34 +489,42 @@
             ref[:, k * LANES : (k + 1) * LANES] = fin[small : small + 1]
             small += 1
 
+    def narrow(j, carry):
+        rows = pl.ds(pl.multiple_of(j * 8, 8), 8)
+        part = turned[pl.ds(pl.multiple_of(j * 8 * th, 8), 8 * th), :]
+        ig_out[rows] = part.reshape(8, th, tw).astype(BF16)
+        return carry
+
+    lax.fori_loop(0, c // 8, narrow, 0)
+
 
 def shards(images, out_grad, conv_weight, proj_weight, gain_one, shift_one, gain_three, shift_three):
     _, _, c, th, tw = images.shape
     co = out_grad.shape[2]
     n_sp, n_bn, n_dp = (lax.axis_size(a) for a in ("sp", "bn", "dp"))
     n_grp, n_pl = n_sp * n_bn, n_bn * n_dp
-    x = images[0, 0].transpose(1, 0, 2)
-    g = out_grad[0, 0].transpose(1, 0, 2)
-    wf = conv_weight.transpose(2, 0, 1, 3).reshape(c, 9 * c)
-    wb = conv_weight[::-1, ::-1].transpose(3, 0, 1, 2).reshape(c, 9 * c)
     rows = 9 * c // 2 + c * (co // LANES) + 1 + 2 * (co // LANES)
     shard = 8 * (-(-rows // (8 * n_pl)))
     vm = pl.BlockSpec(memory_space=pltpu.VMEM)
     dma = pltpu.SemaphoreType.DMA
-    outs = pl.pallas_call(
+    any_space = pl.BlockSpec(memory_space=pl.ANY)
+    ig, fin = pl.pallas_call(
         functools.partial(kernel, n_sp, n_bn, n_dp),
         out_shape=(
             jax.ShapeDtypeStruct((th, c, tw), BF16),
-            jax.ShapeDtypeStruct((9 * c, c), F32),
-            jax.ShapeDtypeStruct((c, co), F32),
-            jax.ShapeDtypeStruct((1, c), F32),
-            jax.ShapeDtypeStruct((1, c), F32),
-            jax.ShapeDtypeStruct((1, co), F32),
-            jax.ShapeDtypeStruct((1, co), F32),
+            jax.ShapeDtypeStruct((n_pl * shard, LANES), F32),
         ),
-        in_specs=[vm] * 8,
-        out_specs=(vm,) * 7,
+        in_specs=[any_space, any_space] + [vm] * 6,
+        out_specs=(vm, vm),
         scratch_shapes=[
+            pltpu.VMEM((c, th, tw), BF16),
+            pltpu.VMEM((co, th, tw), BF16),
+            pltpu.VMEM((c * th, tw), F32),
+            pltpu.VMEM((co * th, tw), F32),
+            dma, dma,
+            pltpu.VMEM((c, 9 * c), BF16),
+            pltpu.VMEM((c, 9 * c), BF16),
+            pltpu.VMEM((co, c), BF16),
             pltpu.VMEM((th + 2, 3 * c, tw), BF16),
             pltpu.VMEM((th + 2, 3 * c, tw), BF16),
             pltpu.VMEM((th, c, tw), F32),
@@ -476,12 +536,12 @@
             pltpu.VMEM((9 * c, c), F32),
             pltpu.VMEM((co, c), F32),
             pltpu.VMEM((2, c, tw), BF16),
+            pltpu.VMEM((c, tw), BF16),
             pltpu.VMEM((2, 3, c, tw), BF16),
             pltpu.VMEM((4, n_grp, 8, co), F32),
             pltpu.VMEM((n_pl * shard, LANES), F32),
             pltpu.VMEM((n_pl, shard, LANES), F32),
             pltpu.VMEM((n_sp, shard, LANES), F32),
-            pltpu.VMEM((n_pl * shard, LANES), F32),
             dma((2, 3)), dma((2, 3)),
             dma((4, n_grp)), dma((4, n_grp)),
             dma((n_pl,)), dma((n_pl,)),
@@ -493,12 +553,27 @@
         ),
         name="branch_step",
     )(
-        x, g, wf, wb, proj_weight.T, proj_weight,
-        jnp.stack([gain_one, shift_one]), jnp.stack([gain_three, shift_three]),
+        images[0, 0], out_grad[0, 0], conv_weight.reshape(9, c, c), proj_weight,
+        gain_one[None], shift_one[None], gain_three[None], shift_three[None],
     )
-    ig, cg, pg, q1, s1, q3, s3 = outs
+    ig, cg, pg, q1, s1, q3, s3 = pl.pallas_call(
+        finish_kernel,
+        out_shape=(
+            jax.ShapeDtypeStruct((c, th, tw), BF16),
+            jax.ShapeDtypeStruct((9 * c, c), F32),
+            jax.ShapeDtypeStruct((c, co), F32),
+            jax.ShapeDtypeStruct((1, c), F32),
+            jax.ShapeDtypeStruct((1, c), F32),
+            jax.ShapeDtypeStruct((1, co), F32),
+            jax.ShapeDtypeStruct((1, co), F32),
+        ),
+        in_specs=[vm] * 2,
+        out_specs=(vm,) * 7,
+        scratch_shapes=[pltpu.VMEM((c * th, tw), F32)],
+        name="unpack",
+    )(ig, fin)
     return (
-        ig.transpose(1, 0, 2)[None, None],
+        ig[None, None],
         cg.reshape(conv_weight.shape),
         pg, q1[0], s1[0], q3[0], s3[0],
     )

time: 99.4 us -> 76 us (0.76)
  local copies, waits for them, and re-layouts: 21.2 us -> 0 us
  other arithmetic: 2.53 us -> 0 us
    unnamed x10 -> x0, local copies, waits for them, and re-layouts: 17.7 us -> none
    pallas_call x0 -> x1, Pallas kernels: none -> 2.71 us  [shards(): pl.pallas_call(finish_kernel, out_shape=(jax.ShapeDtypeStruct((c, th, tw)...]
    another operation x2 -> x0, other arithmetic: 2.53 us -> none  [the longest x1 1.29 us: shards(): jnp.stack([gain_three, shift_three])]
    pallas_call x1, Pallas kernels: 74.5 us -> 72.5 us  [shards(): pl.pallas_call(functools.partial(kernel, n_sp, n_bn, n_dp), out_shape=(ja...]
    reshape x2 -> x0, local copies, waits for them, and re-layouts: 1.53 us -> none  [the longest x1 0.77 us: shards(): wf = conv_weight.transpose(2, 0, 1, 3).reshape(c, 9 * c)]
    transpose x1 -> x0, local copies, waits for them, and re-layouts: 1.05 us -> none  [shards(): wf = conv_weight.transpose(2, 0, 1, 3).reshape(c, 9 * c)]
where the time goes in v2:
time: 76 us; the launch traced here: 75.8 us
  Pallas kernels  75.2 us (99%)
    pallas_call x1, Pallas kernels, shards(): pl.pallas_call(functools.partial(kernel, n_sp, n_bn, n_dp), out_shape=(ja...  72.5 us
    pallas_call x1, Pallas kernels, shards(): pl.pallas_call(finish_kernel, out_shape=(jax.ShapeDtypeStruct((c, th, tw)...  2.71 us

profile of v2, /device:TPU:0, one launch (start us, length us, event | category | flops | bytes accessed | tf_op | source)
XLA Modules:
  0.0 75.8 jit_solution(13329976136687569035)
XLA Ops:
  0.6 72.5 %branch_step.1 = (bf16[40,64,128]{2,1,0:T(8,128)(2,1)}, f32[448,128]{1,0:T(8,128)}) custom-call(bf16[64,40,128]{2,1,0:T(8,128)(2,1)} %bitcast.14, bf16[256,40,128]{2,1,0:T(8,128)(2,1)} %bitcast.13, bf16[9,64,64]{2,1,0:T(8,128)(2,1)} %bitcast.15, bf16[64,256]{1,0:T(8,128)(2,1)} %wp_ref.1, f32[1,64]{1,0:T(1,128)} %bitcast.18, f32[1,64]{1,0:T(1,128)} %bitcast.19, ...), custom_call_target="tpu_custom_call" | custom-call | tf_op jit(solution)/shard_map/branch_step/pallas_call | solution.py:511
  73.1 2.7 %unpack.1 = (bf16[64,40,128]{2,1,0:T(8,128)(2,1)}, f32[576,64]{1,0:T(8,128)}, f32[64,256]{1,0:T(8,128)}, f32[1,64]{1,0:T(1,128)}, f32[1,64]{1,0:T(1,128)}, /*index=5*/f32[1,256]{1,0:T(1,128)}, f32[1,256]{1,0:T(1,128)}) custom-call(bf16[40,64,128]{2,1,0:T(8,128)(2,1)} %get-tuple-element.16.ig_in, f32[448,128]{1,0:T(8,128)} %get-tuple-element.17.fin), custom_call_target="tpu_custom_call" | custom-call | tf_op jit(solution)/shard_map/unpack/pallas_call | solution.py:559

commit v3 on v2

--- a/solution.py
+++ b/solution.py
@@ -34,11 +34,11 @@
 def kernel(
     n_sp, n_bn, n_dp,
     x_hbm, g_hbm, cw_ref, wp_ref, gain1_ref, shift1_ref, gain3_ref, shift3_ref,
-    ig_ref, fin,
+    ig_ref, fin, vec_out,
     x_raw, g_raw, xf, gf, x_sem, g_sem, wf_ref, wb_ref, wpt_ref,
     xs, ds, a_buf, e1_buf, b_buf, e3_buf, y_buf, acc, cgt, gpt,
-    packed, edge_x, halo, stats, rs_send, rs_recv, line,
-    h_send, h_recv, st_send, st_recv, rs_ss, rs_rs, ln_ss, ln_rs, ag_ss, ag_rs,
+    packed, edge_x, halo, stats, rs_send, rs_recv, line, vec,
+    h_send, h_recv, st_send, st_recv, rs_ss, rs_rs, ln_ss, ln_rs, ag_ss, ag_rs, vec_ss, vec_rs,
 ):
     c, th, tw = x_raw.shape
     co = g_raw.shape[0]
@@ -137,12 +137,15 @@
 
     def exchange(k, first, second, meanwhile):
         n = first.shape[1]
-        stats[k, me_g, 0:1, 0:n] = first
-        stats[k, me_g, 1:2, 0:n] = second
+        both = jnp.concatenate([first, second], axis=1)
+        used = 2 * n // LANES
+        for r in range(used):
+            stats[k, me_g, r : r + 1] = both[:, r * LANES : (r + 1) * LANES]
+        rows = pl.ds(0, used)
 
         def copy_to(d):
             return pltpu.make_async_remote_copy(
-                src_ref=stats.at[k, me_g], dst_ref=stats.at[k, me_g],
+                src_ref=stats.at[k, me_g, rows], dst_ref=stats.at[k, me_g, rows],
                 send_sem=st_send.at[k, d], recv_sem=st_recv.at[k, d],
                 device_id=group_peer(d), device_id_type=MESH,
             )
@@ -154,7 +157,7 @@
         def finish(d, carry):
             src = (me_g + n_grp - d) % n_grp
             arrival = pltpu.make_async_remote_copy(
-                src_ref=stats.at[k, me_g], dst_ref=stats.at[k, src],
+                src_ref=stats.at[k, me_g, rows], dst_ref=stats.at[k, src, rows],
                 send_sem=st_send.at[k, d], recv_sem=st_recv.at[k, d],
                 device_id=group_peer(d), device_id_type=MESH,
             )
@@ -165,8 +168,11 @@
         lax.fori_loop(1, n_grp, start, 0)
         meanwhile()
         lax.fori_loop(1, n_grp, finish, 0)
-        firsts = [stats[k, j, 0:1, 0:n] for j in range(n_grp)]
-        seconds = [stats[k, j, 1:2, 0:n] for j in range(n_grp)]
+        firsts, seconds = [], []
+        for j in range(n_grp):
+            flat = jnp.concatenate([stats[k, j, r : r + 1] for r in range(used)], axis=1)
+            firsts.append(flat[:, :n])
+            seconds.append(flat[:, n:])
         return firsts, seconds
 
     def moments(k, mean_row, square_row, meanwhile):
@@ -355,6 +361,20 @@
     local_s1 = row_sum(ssum)
     local_q1 = row_sum(scross)
     full_s1, full_q1 = sums(3, local_s1, local_q1, lambda: None)
+    vec[dp] = jnp.zeros(vec.shape[1:], F32)
+    flat_vec = jnp.concatenate([full_q1, full_s1, full_q3, full_s3], axis=1)
+    n_vec = flat_vec.shape[1] // LANES
+    for r in range(n_vec):
+        vec[dp, r : r + 1] = flat_vec[:, r * LANES : (r + 1) * LANES]
+
+    def vec_copy(d, slot):
+        return pltpu.make_async_remote_copy(
+            src_ref=vec.at[dp], dst_ref=vec.at[slot], send_sem=vec_ss.at[d], recv_sem=vec_rs.at[d],
+            device_id={"sp": sp, "bn": bn, "dp": (dp + d) % n_dp}, device_id_type=MESH,
+        )
+
+    for d in range(1, n_dp):
+        vec_copy(d, dp).start()
     d_a = to_col(gain1 * s1)
     d_s = to_col(full_s1 / cells)
     d_q = to_col(full_q1 / cells)
@@ -381,22 +401,17 @@
     lax.fori_loop(0, th // r8, grad_step, 0)
     half = 9 * c // 2
     flat = jnp.concatenate([cgt[k * c : (k + 1) * c, :].T for k in range(9)], axis=0)
-    rs_send[0:half] = jnp.concatenate([flat[:half], flat[half:]], axis=1)
+    rs_send[0:half] = jnp.concatenate([flat[:half], flat[half:]], axis=1).astype(BF16)
     gp = gpt[...].T
     base = half
     for k in range(co // LANES):
-        rs_send[base : base + c] = gp[:, k * LANES : (k + 1) * LANES]
+        rs_send[base : base + c] = gp[:, k * LANES : (k + 1) * LANES].astype(BF16)
         base += c
-    rs_send[base:] = jnp.zeros((rs_send.shape[0] - base, LANES), F32)
-    rs_send[base : base + 1] = jnp.concatenate([local_q1, local_s1], axis=1)
-    small = base + 1
-    for v in (local_q3, local_s3):
-        for k in range(co // LANES):
-            rs_send[small : small + 1] = v[:, k * LANES : (k + 1) * LANES]
-            small += 1
+    if base < rs_send.shape[0]:
+        rs_send[base:] = jnp.zeros((rs_send.shape[0] - base, LANES), BF16)
 
     def span(p):
-        return pl.ds(pl.multiple_of(p * shard, 8), shard)
+        return pl.ds(pl.multiple_of(p * shard, 16), shard)
 
     def rs_copy(d):
         p, where = plane_peer(d)
@@ -425,9 +440,9 @@
 
     def rs_wait(d, got):
         rs_copy(d).wait()
-        return got + rs_recv[d]
-
-    line[sp] = lax.fori_loop(1, n_pl, rs_wait, rs_send[span(me_p)])
+        return got + rs_recv[d].astype(F32)
+
+    line[sp] = lax.fori_loop(1, n_pl, rs_wait, rs_send[span(me_p)].astype(F32)).astype(BF16)
 
     def ln_copy(d, slot):
         return pltpu.make_async_remote_copy(
@@ -441,10 +456,10 @@
     lax.fori_loop(0, middle, field_step, 0)
     for d in range(1, n_sp):
         ln_copy(d, (sp + n_sp - d) % n_sp).wait()
-    whole = line[0]
+    whole = line[0].astype(F32)
     for k in range(1, n_sp):
-        whole = whole + line[k]
-    fin[span(me_p)] = whole * factor
+        whole = whole + line[k].astype(F32)
+    fin[span(me_p)] = (whole * factor).astype(BF16)
 
     def ag_copy(d, slot):
         return pltpu.make_async_remote_copy(
@@ -463,9 +478,15 @@
     lax.fori_loop(1, n_pl, ag_start, 0)
     lax.fori_loop(middle, th // r4, field_step, 0)
     lax.fori_loop(1, n_pl, ag_wait, 0)
-
-
-def finish_kernel(ig_in, fin, ig_out, cg_out, pg_out, q1_out, s1_out, q3_out, s3_out, turned):
+    for d in range(1, n_dp):
+        vec_copy(d, (dp + n_dp - d) % n_dp).wait()
+    vec_sum = vec[0]
+    for k in range(1, n_dp):
+        vec_sum = vec_sum + vec[k]
+    vec_out[...] = vec_sum * factor
+
+
+def finish_kernel(ig_in, fin, vec, ig_out, cg_out, pg_out, q1_out, s1_out, q3_out, s3_out, turned):
     th, c, tw = ig_in.shape
     co = pg_out.shape[1]
 
@@ -475,18 +496,18 @@
 
     lax.fori_loop(0, th, step, 0)
     half = 9 * c // 2
-    cg_out[0:half] = fin[0:half, 0:c]
-    cg_out[half:] = fin[0:half, c : 2 * c]
+    cg_out[0:half] = fin[0:half, 0:c].astype(F32)
+    cg_out[half:] = fin[0:half, c : 2 * c].astype(F32)
     base = half
     for k in range(co // LANES):
-        pg_out[:, k * LANES : (k + 1) * LANES] = fin[base : base + c]
+        pg_out[:, k * LANES : (k + 1) * LANES] = fin[base : base + c].astype(F32)
         base += c
-    q1_out[...] = fin[base : base + 1, 0:c]
-    s1_out[...] = fin[base : base + 1, c : 2 * c]
-    small = base + 1
+    q1_out[...] = vec[0:1, 0:c]
+    s1_out[...] = vec[0:1, c : 2 * c]
+    small = 1
     for ref in (q3_out, s3_out):
         for k in range(co // LANES):
-            ref[:, k * LANES : (k + 1) * LANES] = fin[small : small + 1]
+            ref[:, k * LANES : (k + 1) * LANES] = vec[small : small + 1]
             small += 1
 
     def narrow(j, carry):
@@ -503,19 +524,21 @@
     co = out_grad.shape[2]
     n_sp, n_bn, n_dp = (lax.axis_size(a) for a in ("sp", "bn", "dp"))
     n_grp, n_pl = n_sp * n_bn, n_bn * n_dp
-    rows = 9 * c // 2 + c * (co // LANES) + 1 + 2 * (co // LANES)
-    shard = 8 * (-(-rows // (8 * n_pl)))
+    rows = 9 * c // 2 + c * (co // LANES)
+    shard = 16 * (-(-rows // (16 * n_pl)))
+    vec_rows = 8 * (-(-(2 * c + 2 * co) // (8 * LANES)))
     vm = pl.BlockSpec(memory_space=pltpu.VMEM)
     dma = pltpu.SemaphoreType.DMA
     any_space = pl.BlockSpec(memory_space=pl.ANY)
-    ig, fin = pl.pallas_call(
+    ig, fin, vec = pl.pallas_call(
         functools.partial(kernel, n_sp, n_bn, n_dp),
         out_shape=(
             jax.ShapeDtypeStruct((th, c, tw), BF16),
-            jax.ShapeDtypeStruct((n_pl * shard, LANES), F32),
+            jax.ShapeDtypeStruct((n_pl * shard, LANES), BF16),
+            jax.ShapeDtypeStruct((vec_rows, LANES), F32),
         ),
         in_specs=[any_space, any_space] + [vm] * 6,
-        out_specs=(vm, vm),
+        out_specs=(vm,) * 3,
         scratch_shapes=[
             pltpu.VMEM((c, th, tw), BF16),
             pltpu.VMEM((co, th, tw), BF16),
@@ -538,15 +561,17 @@
             pltpu.VMEM((2, c, tw), BF16),
             pltpu.VMEM((c, tw), BF16),
             pltpu.VMEM((2, 3, c, tw), BF16),
-            pltpu.VMEM((4, n_grp, 8, co), F32),
-            pltpu.VMEM((n_pl * shard, LANES), F32),
-            pltpu.VMEM((n_pl, shard, LANES), F32),
-            pltpu.VMEM((n_sp, shard, LANES), F32),
+            pltpu.VMEM((4, n_grp, max(8, 2 * co // LANES), LANES), F32),
+            pltpu.VMEM((n_pl * shard, LANES), BF16),
+            pltpu.VMEM((n_pl, shard, LANES), BF16),
+            pltpu.VMEM((n_sp, shard, LANES), BF16),
+            pltpu.VMEM((n_dp, vec_rows, LANES), F32),
             dma((2, 3)), dma((2, 3)),
             dma((4, n_grp)), dma((4, n_grp)),
             dma((n_pl,)), dma((n_pl,)),
             dma((n_sp,)), dma((n_sp,)),
             dma((n_pl,)), dma((n_pl,)),
+            dma((n_dp,)), dma((n_dp,)),
         ],
         compiler_params=pltpu.CompilerParams(
             collective_id=0, has_side_effects=True, vmem_limit_bytes=60 * 1024 * 1024
@@ -567,11 +592,11 @@
             jax.ShapeDtypeStruct((1, co), F32),
             jax.ShapeDtypeStruct((1, co), F32),
         ),
-        in_specs=[vm] * 2,
+        in_specs=[vm] * 3,
         out_specs=(vm,) * 7,
         scratch_shapes=[pltpu.VMEM((c * th, tw), F32)],
         name="unpack",
-    )(ig, fin)
+    )(ig, fin, vec)
     return (
         ig[None, None],
         cg.reshape(conv_weight.shape),

time: 76 us -> 75.2 us (0.989)
  Pallas kernels: 75.2 us -> 74.3 us
    pallas_call x1, Pallas kernels: 72.5 us -> 71.6 us  [shards(): pl.pallas_call(functools.partial(kernel, n_sp, n_bn, n_dp), out_shape=(ja...]
where the time goes in v3:
time: 75.2 us; the launch traced here: 75 us
  Pallas kernels  74.3 us (99%)
    pallas_call x1, Pallas kernels, shards(): pl.pallas_call(functools.partial(kernel, n_sp, n_bn, n_dp), out_shape=(ja...  71.6 us
    pallas_call x1, Pallas kernels, shards(): pl.pallas_call(finish_kernel, out_shape=(jax.ShapeDtypeStruct((c, th, tw)...  2.72 us

profile of v3, /device:TPU:0, one launch (start us, length us, event | category | flops | bytes accessed | tf_op | source)
XLA Modules:
  0.0 75.0 jit_solution(1875957714077769277)
XLA Ops:
  0.6 71.6 %branch_step.1 = (bf16[40,64,128]{2,1,0:T(8,128)(2,1)}, bf16[512,128]{1,0:T(8,128)(2,1)}, f32[8,128]{1,0:T(8,128)}) custom-call(bf16[64,40,128]{2,1,0:T(8,128)(2,1)} %bitcast.14, bf16[256,40,128]{2,1,0:T(8,128)(2,1)} %bitcast.13, bf16[9,64,64]{2,1,0:T(8,128)(2,1)} %bitcast.15, bf16[64,256]{1,0:T(8,128)(2,1)} %wp_ref.1, f32[1,64]{1,0:T(1,128)} %bitcast.18, ...), custom_call_target="tpu_custom_call" | custom-call | tf_op jit(solution)/shard_map/branch_step/pallas_call | solution.py:533
  72.3 2.7 %unpack.1 = (bf16[64,40,128]{2,1,0:T(8,128)(2,1)}, f32[576,64]{1,0:T(8,128)}, f32[64,256]{1,0:T(8,128)}, f32[1,64]{1,0:T(1,128)}, f32[1,64]{1,0:T(1,128)}, /*index=5*/f32[1,256]{1,0:T(1,128)}, f32[1,256]{1,0:T(1,128)}) custom-call(bf16[40,64,128]{2,1,0:T(8,128)(2,1)} %get-tuple-element.17.ig_in, bf16[512,128]{1,0:T(8,128)(2,1)} %get-tuple-element.18.fin, ...), custom_call_target="tpu_custom_call" | custom-call | tf_op jit(solution)/shard_map/unpack/pallas_call | solution.py:584
